TPU v7x, 128 devices: a whole 4x4x4 slice. The times are simulated.
128 devices in a mesh: orb: 128 (over z, x, y, core).
Axes of the slice: x: 4, y: 4, z: 4, core: 2. Of those that a mesh axis runs over, the one named last changes fastest.
Arguments:
- slabs: float32 [256, 384, 768], P('orb'), may hold values from -1.2 to 1.2
- amplitudes: float32 [1024, 384, 384], P('orb'), may hold values from -6 to 6
- intersections: float32 [1024, 3, 384, 384], P('orb'), may hold values from -0.3125 to 0.3125
- fock_coupling: float32 [1024, 3], P('orb'), may hold values from -0.9 to 0.9
- virt_energy: float32 [1024, 384], P('orb'), may hold values from 0.4 to 4
- occ_pair_energy: float32 [1024], P('orb'), may hold values from -2.4 to -0.4
- pair_orbs: int32 [1024, 2], P('orb'), may hold values from 0 to 255, as said below
- couplings: int32 [1024, 3], P('orb'), may hold values from 0 to 1023, as said below
Outputs:
- updated_amplitudes: float32 [1024, 384, 384], P('orb')
Inputs may be any that keep to these rules, and one draw needn't show every extreme that they name: `pair_orbs`: row p holds orbitals (i, j), i != j. A device's block of 8 rows has i among that device's own 2 orbitals (rows of its block of slabs) and j among the orbitals of a device at most 2 away along the axis, counted without wrapping (the first and last devices are not neighbours here); every device's block names orbitals of some device 2 away and of some device next to it. `couplings`: entry (p, c) is a pair coupled to pair p. For c = 0 it is a pair in the block of the device before p's owner, and for c = 1 a pair in the block of the device after it. The axis closes: before the first device comes the last one, and after the last comes the first. Over one device's block of 8 rows, column 0 names exactly 4 distinct pairs, and so does column 1. For c = 2 it is another pair of p's own block.
All inputs are finite; a program needn't handle non-finite values.
Results may differ from a plain program's by a relative error of at most 0.0001.
Values sent between devices are 32-bit elements; how exact they have to be, the bound alone decides.
A program may use at most 192 MiB of HBM per device.

v0:
```python
import jax
import jax.numpy as jnp
from jax import lax
from jax.sharding import PartitionSpec as P

REACH = 2
ITERS = 2


highest = lax.Precision.HIGHEST


def shifted(value, axis, by):
    peers = lax.axis_size(axis)
    pairs = [(i, i + by) for i in range(peers) if 0 <= i + by < peers]
    return lax.ppermute(value, axis, pairs)


def with_halo(cells, sides, width):
    for axis, dim in sides:
        count = lax.axis_size(axis)
        head = lax.slice_in_dim(cells, 0, width, axis=dim)
        tail = lax.slice_in_dim(cells, cells.shape[dim] - width, cells.shape[dim], axis=dim)
        cells = jnp.concatenate(
            [
                lax.ppermute(tail, axis, [(i, (i + 1) % count) for i in range(count)]),
                cells,
                lax.ppermute(head, axis, [((i + 1) % count, i) for i in range(count)]),
            ],
            axis=dim,
        )
    return cells


def fetch_window(slabs):
    pieces = {0: slabs}
    for distance in range(1, REACH + 1):
        for sign in (1, -1):
            pieces[sign * distance] = shifted(slabs, "orb", sign * distance)
    return jnp.concatenate([pieces[-offset] for offset in range(-REACH, REACH + 1)], axis=0)


def shards(
    slabs,
    amplitudes,
    intersections,
    fock_coupling,
    virt_energy,
    occ_pair_energy,
    pair_orbs,
    couplings,
):
    device = lax.axis_index("orb")
    device_count = lax.axis_size("orb")
    orbitals_here = slabs.shape[0]
    pairs_here = amplitudes.shape[0]
    below = (device - 1 + device_count) % device_count
    above = (device + 1) % device_count
    window = fetch_window(slabs)
    local_first = pair_orbs[:, 0] - device * orbitals_here
    window_second = pair_orbs[:, 1] - (device - REACH) * orbitals_here
    left = jnp.take(slabs, local_first, axis=0)
    right = jnp.take(window, window_second, axis=0)
    integrals = jnp.einsum(
        "paq,pbq->pab", left, right, precision=highest, preferred_element_type=jnp.float32
    )
    denominator = virt_energy[:, :, None] + virt_energy[:, None, :] - occ_pair_energy[:, None, None]
    own_index = pairs_here + couplings[:, 2] - device * pairs_here
    lower_index = couplings[:, 0] - below * pairs_here
    upper_index = 2 * pairs_here + couplings[:, 1] - above * pairs_here
    coupled_index = jnp.stack([lower_index, upper_index, own_index], axis=1)
    current = amplitudes
    for step in range(ITERS):
        nearby = with_halo(current, (("orb", 0),), pairs_here)

        def project_pair(row):
            chosen_rows, gains, intersection = row
            picked = jnp.take(nearby, chosen_rows, axis=0)
            half = jnp.einsum(
                "cab,cbe->cae",
                intersection,
                picked,
                precision=highest,
                preferred_element_type=jnp.float32,
            )
            whole = jnp.einsum(
                "cae,cfe->caf",
                half,
                intersection,
                precision=highest,
                preferred_element_type=jnp.float32,
            )
            return jnp.sum(gains[:, None, None] * whole, axis=0)

        coupled = lax.map(project_pair, (coupled_index, fock_coupling, intersections))
        residual = integrals + denominator * current - coupled
        current = current - residual / denominator
    return current


def solution(mesh):
    in_specs = (
        P("orb", None, None),
        P("orb", None, None),
        P("orb", None, None, None),
        P("orb", None),
        P("orb", None),
        P("orb"),
        P("orb", None),
        P("orb", None),
    )
    out_specs = P("orb", None, None)
    return jax.shard_map(shards, mesh=mesh, in_specs=in_specs, out_specs=out_specs, check_vma=False)
```

profile of v0, /device:TPU:0, one launch (start us, length us, event | category | flops | bytes accessed | tf_op | source)
XLA Modules:
  0.0 535.6 jit_solution(2100506050162996361)
XLA Ops:
  3.8 7.2 %collective-permute-start.5 = (f32[8,384,384]{2,1,0:T(8,128)}, f32[8,384,384]{2,1,0:T(8,128)}, u32[]{:S(2)}, u32[]{:S(2)}) collective-permute-start(f32[8,384,384]{2,1,0:T(8,128)} %param.15), channel_id=1, source_target_pairs={{1,0},{2,1},{3,2},{4,3},{5,4},{6,5},{7,6},{8,7},{9,8},{10,9},{11,1... | collective-permute-start | bytes 14155784 | tf_op jit(solution)/shard_map/ppermute | solution.py:28
  15.0 40.5 %collective-permute-done = f32[2,384,768]{2,1,0:T(8,128)S(1)} collective-permute-done((f32[2,384,768]{2,1,0:T(8,128)}, f32[2,384,768]{2,1,0:T(8,128)S(1)}, u32[]{:S(2)}, u32[]{:S(2)}) %collective-permute-start) | collective-permute-done | bytes 2359328 | tf_op jit(solution)/shard_map/ppermute | solution.py:16
  59.4 6.3 %gather_fusion.2 = f32[8,384,768]{2,1,0:T(8,128)} fusion(f32[2,384,768]{2,1,0:T(8,128)} %param.14, s32[1024]{0:T(1024)S(1)} %get-tuple-element.124), kind=kCustom, calls=%fused_computation.2 | custom fusion | bytes 18874400 | tf_op jit(solution)/shard_map/jit(_take)/gather | solution.py:62
  70.2 65.0 %collective-permute-done.3 = f32[2,384,768]{2,1,0:T(8,128)} collective-permute-done((f32[2,384,768]{2,1,0:T(8,128)}, f32[2,384,768]{2,1,0:T(8,128)}, u32[]{:S(2)}, u32[]{:S(2)}) %collective-permute-start.3) | collective-permute-done | bytes 2359328 | tf_op jit(solution)/shard_map/ppermute | solution.py:16
  141.4 9.2 %gather_fusion.3 = f32[8,384,768]{2,1,0:T(8,128)} fusion(f32[10,384,768]{2,1,0:T(8,128)} %copy-done.2, s32[1024]{0:T(1024)S(1)} %get-tuple-element.123), kind=kCustom, calls=%fused_computation.3 | custom fusion | bytes 18874400 | tf_op jit(solution)/shard_map/jit(_take)/gather | solution.py:63
  150.7 19.8 %fusion.32 = f32[8,384,384]{2,1,0:T(8,128)} fusion(f32[8,384,768]{2,1,0:T(8,128)} %gather_fusion.3, f32[8,384,768]{2,1,0:T(8,128)} %gather_fusion.2, pred[8]{0:T(512)(128)(4,1)S(1)} %get-tuple-element.119, pred[8]{0:T(512)(128)(4,1)S(1)} %get-tuple-element.112), kind=kOutput, calls=%fused_computation.48 | convolution fusion | flops 10876354560 | bytes 23592976 | tf_op jit(solution)/shard_map/paq,pbq->pab/dot_general | solution.py:64
  170.5 9.5 %pad_maximum_fusion = f32[24,384,384]{2,1,0:T(8,128)} fusion(f32[8,384,384]{2,1,0:T(8,128)} %collective-permute-done.5, f32[8,384,384]{2,1,0:T(8,128)S(1)} %bitcast.61, f32[8,384,384]{2,1,0:T(8,128)} %collective-permute-done.4), kind=kLoop, calls=%fused_computation.46 | loop fusion | flops 7077888 | bytes 28311552 | tf_op jit(solution)/shard_map/concatenate | solution.py:24
  182.6 136.0 %while.20 = (s32[]{:T(128)}, f32[8,384,384]{2,1,0:T(8,128)}, f32[8,3]{1,0:T(8,128)S(1)}, f32[8,3,384,384]{3,2,1,0:T(8,128)}, s32[8,3]{1,0:T(8,128)S(1)}, /*index=5*/f32[24,384,384]{2,1,0:T(8,128)}, s32[]{:T(128)}) while((s32[]{:T(128)}, f32[8,384,384]{2,1,0:T(8,128)}, f32[8,3]{1,0:T(8,128)S(1)}, f32[8,3,384,384]{3,2,1,0:T(8,128)}, ...), condition=%wide.region_2.4_spmd, body=%wide.region_0.3_spmd.sunk | while | flops 4078044160 | bytes 14161583 | solution.py:95
  182.6 5.7 %gather_fusion = f32[3,384,384]{2,1,0:T(8,128)S(1)} fusion(f32[24,384,384]{2,1,0:T(8,128)} %get-tuple-element.226, s32[1024]{0:T(1024)S(1)} %pad_clamp_fusion.6), kind=kCustom, calls=%fused_computation.clone.clone.1 | custom fusion | bytes 3538956 | tf_op jit(solution)/shard_map/while/body/eval_jaxpr/jit(_take)/gather | solution.py:78
  188.3 5.2 fusion.58
  199.6 5.7 %gather_fusion = f32[3,384,384]{2,1,0:T(8,128)S(1)} fusion(f32[24,384,384]{2,1,0:T(8,128)} %get-tuple-element.226, s32[1024]{0:T(1024)S(1)} %pad_clamp_fusion.6), kind=kCustom, calls=%fused_computation.clone.clone.1 | custom fusion | bytes 3538956 | tf_op jit(solution)/shard_map/while/body/eval_jaxpr/jit(_take)/gather | solution.py:78
  205.3 5.2 fusion.58
  216.6 5.7 %gather_fusion = f32[3,384,384]{2,1,0:T(8,128)S(1)} fusion(f32[24,384,384]{2,1,0:T(8,128)} %get-tuple-element.226, s32[1024]{0:T(1024)S(1)} %pad_clamp_fusion.6), kind=kCustom, calls=%fused_computation.clone.clone.1 | custom fusion | bytes 3538956 | tf_op jit(solution)/shard_map/while/body/eval_jaxpr/jit(_take)/gather | solution.py:78
  222.3 5.2 fusion.58
  227.5 5.2 multiply_reduce_fusion.4
  233.6 5.7 %gather_fusion = f32[3,384,384]{2,1,0:T(8,128)S(1)} fusion(f32[24,384,384]{2,1,0:T(8,128)} %get-tuple-element.226, s32[1024]{0:T(1024)S(1)} %pad_clamp_fusion.6), kind=kCustom, calls=%fused_computation.clone.clone.1 | custom fusion | bytes 3538956 | tf_op jit(solution)/shard_map/while/body/eval_jaxpr/jit(_take)/gather | solution.py:78
  239.3 5.2 fusion.58
  244.5 5.2 multiply_reduce_fusion.4
  250.6 5.7 %gather_fusion = f32[3,384,384]{2,1,0:T(8,128)S(1)} fusion(f32[24,384,384]{2,1,0:T(8,128)} %get-tuple-element.226, s32[1024]{0:T(1024)S(1)} %pad_clamp_fusion.6), kind=kCustom, calls=%fused_computation.clone.clone.1 | custom fusion | bytes 3538956 | tf_op jit(solution)/shard_map/while/body/eval_jaxpr/jit(_take)/gather | solution.py:78
  256.3 5.2 fusion.58
  267.6 5.7 %gather_fusion = f32[3,384,384]{2,1,0:T(8,128)S(1)} fusion(f32[24,384,384]{2,1,0:T(8,128)} %get-tuple-element.226, s32[1024]{0:T(1024)S(1)} %pad_clamp_fusion.6), kind=kCustom, calls=%fused_computation.clone.clone.1 | custom fusion | bytes 3538956 | tf_op jit(solution)/shard_map/while/body/eval_jaxpr/jit(_take)/gather | solution.py:78
  273.3 5.2 fusion.58
  284.6 5.7 %gather_fusion = f32[3,384,384]{2,1,0:T(8,128)S(1)} fusion(f32[24,384,384]{2,1,0:T(8,128)} %get-tuple-element.226, s32[1024]{0:T(1024)S(1)} %pad_clamp_fusion.6), kind=kCustom, calls=%fused_computation.clone.clone.1 | custom fusion | bytes 3538956 | tf_op jit(solution)/shard_map/while/body/eval_jaxpr/jit(_take)/gather | solution.py:78
  290.3 5.2 fusion.58
  301.6 5.7 %gather_fusion = f32[3,384,384]{2,1,0:T(8,128)S(1)} fusion(f32[24,384,384]{2,1,0:T(8,128)} %get-tuple-element.226, s32[1024]{0:T(1024)S(1)} %pad_clamp_fusion.6), kind=kCustom, calls=%fused_computation.clone.clone.1 | custom fusion | bytes 3538956 | tf_op jit(solution)/shard_map/while/body/eval_jaxpr/jit(_take)/gather | solution.py:78
  307.3 5.2 fusion.58
  318.6 6.0 %divide_subtract_fusion.1 = f32[8,384,384]{2,1,0:T(8,128)S(1)} fusion(f32[8,384,384]{2,1,0:T(8,128)} %param.15, f32[8,384,384]{2,1,0:T(8,128)} %get-tuple-element.70, f32[8,384,384]{2,1,0:T(8,128)} %fusion.32, f32[8]{0:T(128)S(1)} %copy-done.4, f32[8,384]{1,0:T(8,128)S(1)} %copy-done.3), kind=kLoop, calls=%fused_computation.52 | loop fusion | flops 8257536 | bytes 18886688 | tf_op jit(solution)/shard_map/sub | solution.py:97
  324.7 7.2 %collective-permute-start.7 = (f32[8,384,384]{2,1,0:T(8,128)S(1)}, f32[8,384,384]{2,1,0:T(8,128)S(1)}, u32[]{:S(2)}, u32[]{:S(2)}) collective-permute-start(f32[8,384,384]{2,1,0:T(8,128)S(1)} %divide_subtract_fusion.1), channel_id=1, source_target_pairs={{1,0},{2,1},{3,2},{4,3},{5,4},{6,5},{7,6},{8,7},{9,8},{10,9},{11,1... | collective-permute-start | bytes 14155784 | tf_op jit(solution)/shard_map/ppermute | solution.py:28
  331.9 51.8 %collective-permute-done.6 = f32[8,384,384]{2,1,0:T(8,128)S(1)} collective-permute-done((f32[8,384,384]{2,1,0:T(8,128)S(1)}, f32[8,384,384]{2,1,0:T(8,128)S(1)}, u32[]{:S(2)}, u32[]{:S(2)}) %collective-permute-start.6) | collective-permute-done | bytes 4718624 | tf_op jit(solution)/shard_map/ppermute | solution.py:26
  383.7 5.3 pad_maximum_fusion.1
  391.5 136.1 %while.21 = (s32[]{:T(128)}, f32[8,384,384]{2,1,0:T(8,128)}, f32[8,3]{1,0:T(8,128)S(1)}, f32[8,3,384,384]{3,2,1,0:T(8,128)}, s32[8,3]{1,0:T(8,128)S(1)}, /*index=5*/f32[24,384,384]{2,1,0:T(8,128)}, s32[]{:T(128)}) while((s32[]{:T(128)}, f32[8,384,384]{2,1,0:T(8,128)}, f32[8,3]{1,0:T(8,128)S(1)}, f32[8,3,384,384]{3,2,1,0:T(8,128)}, ...), condition=%wide.region_5.7_spmd, body=%wide.region_3.6_spmd.sunk | while | flops 4078044160 | bytes 14161583 | solution.py:95
  391.5 5.7 %gather_fusion.1 = f32[3,384,384]{2,1,0:T(8,128)S(1)} fusion(f32[24,384,384]{2,1,0:T(8,128)} %get-tuple-element.247, s32[1024]{0:T(1024)S(1)} %pad_clamp_fusion.7), kind=kCustom, calls=%fused_computation.1.clone.clone.1 | custom fusion | bytes 3538956 | tf_op jit(solution)/shard_map/while/body/eval_jaxpr/jit(_take)/gather | solution.py:78
  397.2 5.2 fusion.64
  408.6 5.7 %gather_fusion.1 = f32[3,384,384]{2,1,0:T(8,128)S(1)} fusion(f32[24,384,384]{2,1,0:T(8,128)} %get-tuple-element.247, s32[1024]{0:T(1024)S(1)} %pad_clamp_fusion.7), kind=kCustom, calls=%fused_computation.1.clone.clone.1 | custom fusion | bytes 3538956 | tf_op jit(solution)/shard_map/while/body/eval_jaxpr/jit(_take)/gather | solution.py:78
  414.3 5.2 fusion.64
  425.6 5.7 %gather_fusion.1 = f32[3,384,384]{2,1,0:T(8,128)S(1)} fusion(f32[24,384,384]{2,1,0:T(8,128)} %get-tuple-element.247, s32[1024]{0:T(1024)S(1)} %pad_clamp_fusion.7), kind=kCustom, calls=%fused_computation.1.clone.clone.1 | custom fusion | bytes 3538956 | tf_op jit(solution)/shard_map/while/body/eval_jaxpr/jit(_take)/gather | solution.py:78
  431.3 5.2 fusion.64
  442.6 5.7 %gather_fusion.1 = f32[3,384,384]{2,1,0:T(8,128)S(1)} fusion(f32[24,384,384]{2,1,0:T(8,128)} %get-tuple-element.247, s32[1024]{0:T(1024)S(1)} %pad_clamp_fusion.7), kind=kCustom, calls=%fused_computation.1.clone.clone.1 | custom fusion | bytes 3538956 | tf_op jit(solution)/shard_map/while/body/eval_jaxpr/jit(_take)/gather | solution.py:78
  448.3 5.2 fusion.64
  459.6 5.7 %gather_fusion.1 = f32[3,384,384]{2,1,0:T(8,128)S(1)} fusion(f32[24,384,384]{2,1,0:T(8,128)} %get-tuple-element.247, s32[1024]{0:T(1024)S(1)} %pad_clamp_fusion.7), kind=kCustom, calls=%fused_computation.1.clone.clone.1 | custom fusion | bytes 3538956 | tf_op jit(solution)/shard_map/while/body/eval_jaxpr/jit(_take)/gather | solution.py:78
  465.3 5.2 fusion.64
  476.6 5.7 %gather_fusion.1 = f32[3,384,384]{2,1,0:T(8,128)S(1)} fusion(f32[24,384,384]{2,1,0:T(8,128)} %get-tuple-element.247, s32[1024]{0:T(1024)S(1)} %pad_clamp_fusion.7), kind=kCustom, calls=%fused_computation.1.clone.clone.1 | custom fusion | bytes 3538956 | tf_op jit(solution)/shard_map/while/body/eval_jaxpr/jit(_take)/gather | solution.py:78
  482.3 5.2 fusion.64
  493.6 5.7 %gather_fusion.1 = f32[3,384,384]{2,1,0:T(8,128)S(1)} fusion(f32[24,384,384]{2,1,0:T(8,128)} %get-tuple-element.247, s32[1024]{0:T(1024)S(1)} %pad_clamp_fusion.7), kind=kCustom, calls=%fused_computation.1.clone.clone.1 | custom fusion | bytes 3538956 | tf_op jit(solution)/shard_map/while/body/eval_jaxpr/jit(_take)/gather | solution.py:78
  499.3 5.2 fusion.64
  510.7 5.7 %gather_fusion.1 = f32[3,384,384]{2,1,0:T(8,128)S(1)} fusion(f32[24,384,384]{2,1,0:T(8,128)} %get-tuple-element.247, s32[1024]{0:T(1024)S(1)} %pad_clamp_fusion.7), kind=kCustom, calls=%fused_computation.1.clone.clone.1 | custom fusion | bytes 3538956 | tf_op jit(solution)/shard_map/while/body/eval_jaxpr/jit(_take)/gather | solution.py:78
  516.3 5.2 fusion.64
  527.6 8.0 %divide_subtract_fusion = f32[8,384,384]{2,1,0:T(8,128)} fusion(f32[8,384,384]{2,1,0:T(8,128)} %copy-done.1, f32[8,384,384]{2,1,0:T(8,128)} %get-tuple-element.71, f32[8,384,384]{2,1,0:T(8,128)} %fusion.32, f32[8]{0:T(128)S(1)} %copy-done.4, f32[8,384]{1,0:T(8,128)S(1)} %copy-done.3), kind=kLoop, calls=%fused_computation.51 | loop fusion | flops 8257536 | bytes 18886688 | tf_op jit(solution)/shard_map/sub | solution.py:97
  (121 shorter events, 114.3 us)
Async XLA Ops:
  0.0 55.5 %collective-permute-start = (f32[2,384,768]{2,1,0:T(8,128)}, f32[2,384,768]{2,1,0:T(8,128)S(1)}, u32[]{:S(2)}, u32[]{:S(2)}) collective-permute-start(f32[2,384,768]{2,1,0:T(8,128)} %param.14), channel_id=1, source_target_pairs={{0,2},{1,3},{2,4},{3,5},{4,6},{5,7},{6,8},{7,9},{8,10},{9,11},{10,... | collective-permute-start | bytes 7077896 | tf_op jit(solution)/shard_map/ppermute | solution.py:16
  3.7 166.7 %collective-permute-start.4 = (f32[8,384,384]{2,1,0:T(8,128)}, f32[8,384,384]{2,1,0:T(8,128)}, u32[]{:S(2)}, u32[]{:S(2)}) collective-permute-start(f32[8,384,384]{2,1,0:T(8,128)} %param.15), channel_id=1, source_target_pairs={{0,1},{1,2},{2,3},{3,4},{4,5},{5,6},{6,7},{7,8},{8,9},{9,10},{10,1... | collective-permute-start | bytes 14155784 | tf_op jit(solution)/shard_map/ppermute | solution.py:26
  3.8 166.6 %collective-permute-start.5 = (f32[8,384,384]{2,1,0:T(8,128)}, f32[8,384,384]{2,1,0:T(8,128)}, u32[]{:S(2)}, u32[]{:S(2)}) collective-permute-start(f32[8,384,384]{2,1,0:T(8,128)} %param.15), channel_id=1, source_target_pairs={{1,0},{2,1},{3,2},{4,3},{5,4},{6,5},{7,6},{8,7},{9,8},{10,9},{11,1... | collective-permute-start | bytes 14155784 | tf_op jit(solution)/shard_map/ppermute | solution.py:28
  11.0 55.0 %collective-permute-start.1 = (f32[2,384,768]{2,1,0:T(8,128)}, f32[2,384,768]{2,1,0:T(8,128)}, u32[]{:S(2)}, u32[]{:S(2)}) collective-permute-start(f32[2,384,768]{2,1,0:T(8,128)} %param.14), channel_id=1, source_target_pairs={{0,1},{1,2},{2,3},{3,4},{4,5},{5,6},{6,7},{7,8},{8,9},{9,10},{10,1... | collective-permute-start | bytes 7077896 | tf_op jit(solution)/shard_map/ppermute | solution.py:16
  13.7 54.7 %collective-permute-start.2 = (f32[2,384,768]{2,1,0:T(8,128)}, f32[2,384,768]{2,1,0:T(8,128)}, u32[]{:S(2)}, u32[]{:S(2)}) collective-permute-start(f32[2,384,768]{2,1,0:T(8,128)} %param.14), channel_id=1, source_target_pairs={{1,0},{2,1},{3,2},{4,3},{5,4},{6,5},{7,6},{8,7},{9,8},{10,9},{11,1... | collective-permute-start | bytes 7077896 | tf_op jit(solution)/shard_map/ppermute | solution.py:16
  55.5 79.7 %collective-permute-start.3 = (f32[2,384,768]{2,1,0:T(8,128)}, f32[2,384,768]{2,1,0:T(8,128)}, u32[]{:S(2)}, u32[]{:S(2)}) collective-permute-start(f32[2,384,768]{2,1,0:T(8,128)} %param.14), channel_id=1, source_target_pairs={{2,0},{3,1},{4,2},{5,3},{6,4},{7,5},{8,6},{9,7},{10,8},{11,9},{12,... | collective-permute-start | bytes 7077896 | tf_op jit(solution)/shard_map/ppermute | solution.py:16
  65.8 2.4 copy-start
  137.1 4.4 copy-start.2
  141.4 29.0 %slice-start = ((s8[4718592]{0:T(1024)(128)(4,1)}), s8[524288]{0:T(1024)(128)(4,1)S(1)}, s32[]{:S(2)}) async-start(s8[4718592]{0:T(1024)(128)(4,1)} %bitcast.60), calls=%async_computation | async-start | bytes 1048576
  150.6 19.8 %slice-start.1 = ((s8[4718592]{0:T(1024)(128)(4,1)}), s8[4194304]{0:T(1024)(128)(4,1)S(1)}, s32[]{:S(2)}) async-start(s8[4718592]{0:T(1024)(128)(4,1)} %bitcast.60), calls=%async_computation.1 | async-start | bytes 8388608
  182.6 136.0 %copy-start.3 = (f32[8,384]{1,0:T(8,128)S(1)}, f32[8,384]{1,0:T(8,128)}, u32[]{:S(2)}) copy-start(f32[8,384]{1,0:T(8,128)} %param.18) | copy-start | bytes 36868
  182.6 136.0 %copy-start.4 = (f32[8]{0:T(128)S(1)}, f32[8]{0:T(128)}, u32[]{:S(2)}) copy-start(f32[8]{0:T(128)} %param.19) | copy-start | bytes 100
  324.6 64.4 %copy-start.1 = (f32[8,384,384]{2,1,0:T(8,128)}, f32[8,384,384]{2,1,0:T(8,128)S(1)}, u32[]{:S(2)}) copy-start(f32[8,384,384]{2,1,0:T(8,128)S(1)} %divide_subtract_fusion.1) | copy-start | bytes 14155780
  324.6 59.0 %collective-permute-start.6 = (f32[8,384,384]{2,1,0:T(8,128)S(1)}, f32[8,384,384]{2,1,0:T(8,128)S(1)}, u32[]{:S(2)}, u32[]{:S(2)}) collective-permute-start(f32[8,384,384]{2,1,0:T(8,128)S(1)} %divide_subtract_fusion.1), channel_id=1, source_target_pairs={{0,1},{1,2},{2,3},{3,4},{4,5},{5,6},{6,7},{7,8},{8,9},{9,10},{10,1... | collective-permute-start | bytes 14155784 | tf_op jit(solution)/shard_map/ppermute | solution.py:26
  324.7 59.0 %collective-permute-start.7 = (f32[8,384,384]{2,1,0:T(8,128)S(1)}, f32[8,384,384]{2,1,0:T(8,128)S(1)}, u32[]{:S(2)}, u32[]{:S(2)}) collective-permute-start(f32[8,384,384]{2,1,0:T(8,128)S(1)} %divide_subtract_fusion.1), channel_id=1, source_target_pairs={{1,0},{2,1},{3,2},{4,3},{5,4},{6,5},{7,6},{8,7},{9,8},{10,9},{11,1... | collective-permute-start | bytes 14155784 | tf_op jit(solution)/shard_map/ppermute | solution.py:28
where the time goes:
time: 542 us; the launch traced here: 536 us
  matrix products  186 us (34%)
  waiting for transfers between devices  157 us (29%)
  local copies, waits for them, and re-layouts  138 us (25%)
  other arithmetic  30 us (6%)
  starting transfers between devices  23.5 us (4%)
    ppermute x4, waiting for transfers between devices, shifted(): return lax.ppermute(value, axis, pairs)  106 us
    gather x16, local copies, waits for them, and re-layouts, project_pair(): picked = jnp.take(nearby, chosen_rows, axis=0)  90.9 us
    dot_general x16, matrix products, project_pair(): jnp.einsum('cab,cbe->cae', intersection, picked, precision=highest, prefe...  83.3 us
    dot_general x16, matrix products, project_pair(): jnp.einsum('cae,cfe->caf', half, intersection, precision=highest, preferr...  83 us
    ppermute x2, waiting for transfers between devices, with_halo(): lax.ppermute(tail, axis, [(i, (i + 1) % count) for i in range(count)])  51.8 us
    dot_general x1, matrix products, shards(): jnp.einsum('paq,pbq->pab', left, right, precision=highest, preferred_elem...  19.8 us
    concatenate x2, other arithmetic, with_halo(): jnp.concatenate([lax.ppermute(tail, axis, [(i, (i + 1) % count) for i in...  14.8 us
    ppermute x2, starting transfers between devices, with_halo(): lax.ppermute(head, axis, [((i + 1) % count, i) for i in range(count)])  14.3 us
  transfers between devices with their start and end apart: 8, of which 3 were waited for; matrix products, arithmetic and copies ran while one was open for 8% of the time, Pallas kernels for 0%

commit v1 on v0

v1 whole, which is shorter than its diff:
```python
import functools

import jax
import jax.numpy as jnp
from jax import lax
from jax.experimental import pallas as pl
from jax.experimental.pallas import tpu as pltpu
from jax.sharding import PartitionSpec as P

MESH = pl.DeviceIdType.MESH
F32 = jnp.float32
BF16 = jnp.bfloat16
NT = (((1,), (1,)), ((), ()))

CUT = 256

IDX_P, IDX_X = 0, 1
SLAB_P = 2
SLAB_A = 4
SLAB_B = 6
SLAB_F = 8
AMP_P = 10
AMP_X = 12
CUR_P = 14
CUR_X = 16
KINDS = 18

OWN, PARTNER, FORWARDED, ACROSS, ACROSS2 = 0, 2, 4, 6, 8


def split(x):
    high = x.astype(BF16)
    return high, (x - high.astype(F32)).astype(BF16)


def dot_nn(a, b):
    return jnp.dot(a, b, preferred_element_type=F32)


def dot_nt(a, b):
    return lax.dot_general(a, b, NT, preferred_element_type=F32)


def transform(gain, full, chunk, first):
    width = chunk.shape[1]
    full_hi, full_lo = split(full)
    chunk_hi, chunk_lo = split(chunk)
    half = gain * dot_nn(
        jnp.concatenate([full_hi, full_hi, full_lo], axis=1),
        jnp.concatenate([chunk_hi, chunk_lo, chunk_hi], axis=0),
    )
    half_hi, half_lo = split(half)
    part_hi = full_hi[:, first : first + width]
    part_lo = full_lo[:, first : first + width]
    return dot_nt(
        jnp.concatenate([half_hi, half_hi, half_lo], axis=1),
        jnp.concatenate([part_hi, part_lo, part_hi], axis=1),
    )


def slab_product(left, right):
    left_hi, left_lo = split(left)
    right_hi, right_lo = split(right)
    return dot_nt(left_hi, right_hi) + dot_nt(left_hi, right_lo) + dot_nt(left_lo, right_hi)


def kernel(
    devices,
    couplings,
    pair_orbs,
    fock,
    occupied,
    virtual,
    slabs,
    amplitudes,
    intersections,
    out,
    cur,
    acc0,
    acc1,
    inter_own,
    inter_p,
    inter_x,
    left,
    win0,
    win1,
    amp_p0,
    amp_p1,
    amp_x0,
    amp_x1,
    cur_p0,
    cur_p1,
    cur_x0,
    cur_x1,
    out_p0,
    out_p1,
    out_x0,
    out_x1,
    idx_p,
    idx_x,
    pick,
    slot,
    send_sem,
    recv_sem,
    local_sem,
    store_sem,
):
    pairs, nv = cur.shape[0], cur.shape[1]
    picks = out_p0.shape[0]
    orbitals = left.shape[0]
    me = lax.axis_index("orb")
    side = 1 - 2 * lax.rem(me, 2)
    partner = me + side
    across = lax.rem(me - side + devices, devices)
    target2 = lax.rem(me + 2 * side + devices, devices)
    source2 = lax.rem(me - 2 * side + devices, devices)
    column_p = lax.rem(me + 1, 2)
    column_x = lax.rem(me, 2)

    local = []

    def fetch(src, dst):
        copy = pltpu.make_async_copy(src, dst, local_sem.at[len(local)])
        local.append(copy)
        copy.start()
        return copy

    get_cur = fetch(amplitudes, cur)
    get_own = fetch(intersections.at[:, 2], inter_own)
    get_p = fetch(intersections.at[:, column_p], inter_p)
    get_left = fetch(slabs, left)
    get_win0 = fetch(slabs.at[:, pl.ds(0, CUT)], win0.at[pl.ds(OWN, orbitals)])
    get_win1 = fetch(slabs.at[:, pl.ds(CUT, nv - CUT)], win1.at[pl.ds(OWN, orbitals)])
    get_x = fetch(intersections.at[:, column_x], inter_x)

    barrier = pltpu.get_barrier_semaphore()
    for other in (partner, across, target2, source2):
        pl.semaphore_signal(barrier, inc=1, device_id=(other,), device_id_type=MESH)
    pl.semaphore_wait(barrier, 4)

    def remote(src, dst, kind, device):
        return pltpu.make_async_remote_copy(
            src_ref=src,
            dst_ref=dst,
            send_sem=send_sem.at[kind],
            recv_sem=recv_sem.at[kind],
            device_id=(device,),
            device_id_type=MESH,
        )

    slab0 = slabs.at[:, pl.ds(0, CUT)]
    slab1 = slabs.at[:, pl.ds(CUT, nv - CUT)]
    rows = lambda first: pl.ds(first, orbitals)
    send_idx_p = remote(couplings, idx_p, IDX_P, partner)
    send_idx_x = remote(couplings, idx_x, IDX_X, across)
    send_p0 = remote(slab0, win0.at[rows(PARTNER)], SLAB_P, partner)
    send_p1 = remote(slab1, win1.at[rows(PARTNER)], SLAB_P + 1, partner)
    send_a0 = remote(slab0, win0.at[rows(ACROSS)], SLAB_A, across)
    send_a1 = remote(slab1, win1.at[rows(ACROSS)], SLAB_A + 1, across)
    send_b0 = remote(slab0, win0.at[rows(ACROSS2)], SLAB_B, target2)
    send_b1 = remote(slab1, win1.at[rows(ACROSS2)], SLAB_B + 1, target2)
    send_f0 = remote(win0.at[rows(ACROSS)], win0.at[rows(FORWARDED)], SLAB_F, partner)
    send_f1 = remote(win1.at[rows(ACROSS)], win1.at[rows(FORWARDED)], SLAB_F + 1, partner)
    send_amp_p0 = remote(out_p0, amp_p0, AMP_P, partner)
    send_amp_p1 = remote(out_p1, amp_p1, AMP_P + 1, partner)
    send_amp_x0 = remote(out_x0, amp_x0, AMP_X, across)
    send_amp_x1 = remote(out_x1, amp_x1, AMP_X + 1, across)
    send_cur_p0 = remote(out_p0, cur_p0, CUR_P, partner)
    send_cur_p1 = remote(out_p1, cur_p1, CUR_P + 1, partner)
    send_cur_x0 = remote(out_x0, cur_x0, CUR_X, across)
    send_cur_x1 = remote(out_x1, cur_x1, CUR_X + 1, across)

    send_idx_x.start()
    send_idx_p.start()
    send_a0.start()
    send_b0.start()
    send_b1.start()
    send_p0.start()
    send_p1.start()

    def tables(source, column, base):
        named = [source[p, column] - base for p in range(pairs)]
        present = []
        for q in range(pairs):
            hit = jnp.int32(0)
            for value in named:
                hit = jnp.maximum(hit, (value == q).astype(jnp.int32))
            present.append(hit)
        below = [jnp.int32(0)]
        for q in range(pairs - 1):
            below.append(below[-1] + present[q])
        return named, present, below

    for row, column, owner in ((0, column_p, partner), (1, column_x, across)):
        named, present, below = tables(couplings, column, owner * pairs)
        for p in range(pairs):
            value = jnp.int32(0)
            for q in range(pairs):
                value = value + jnp.where(named[p] == q, below[q], 0)
            slot[row, p] = jnp.minimum(value, picks - 1)

    send_idx_x.wait_recv()
    send_idx_p.wait_recv()
    for row, column, source in ((0, column_x, idx_p), (1, column_p, idx_x)):
        _, present, below = tables(source, column, me * pairs)
        for s in range(picks):
            value = jnp.int32(0)
            for q in range(pairs):
                chosen = jnp.logical_and(present[q] == 1, below[q] == s)
                value = value + jnp.where(chosen, q, 0)
            pick[row, s] = jnp.minimum(value, pairs - 1)

    def gather(row, dst, first):
        width = dst.shape[2]

        def step(s, carry):
            dst[s] = cur[pick[row, s], :, first : first + width]
            return carry

        lax.fori_loop(0, picks, step, 0)

    get_cur.wait()
    gather(1, out_x0, 0)
    gather(1, out_x1, CUT)
    send_amp_x0.start()
    send_amp_x1.start()
    send_a1.start()
    gather(0, out_p0, 0)
    gather(0, out_p1, CUT)
    send_amp_p0.start()
    send_amp_p1.start()

    def each_pair(step):
        def body(p, carry):
            step(p)
            return carry

        lax.fori_loop(0, pairs, body, 0)

    def third(p):
        return jnp.clip(couplings[p, 2] - me * pairs, 0, pairs - 1)

    get_own.wait()

    def own_first(p):
        chosen = cur[third(p)]
        acc0[p] = transform(fock[p, 2], inter_own[p], chosen, 0)

    each_pair(own_first)

    get_p.wait()
    send_amp_p0.wait_recv()
    send_amp_p1.wait_recv()

    def partner_first(p):
        q = slot[0, p]
        chosen = jnp.concatenate([amp_p0[q], amp_p1[q]], axis=1)
        acc0[p] += transform(fock[p, column_p], inter_p[p], chosen, 0)

    each_pair(partner_first)

    def second(p):
        offset = lax.div(pair_orbs[p, 1], orbitals) - me
        parity = lax.rem(pair_orbs[p, 1], orbitals)
        turned = offset * side
        place = jnp.where(turned >= 0, turned, 2 - turned)
        return jnp.clip(place * orbitals + parity, 0, win0.shape[0] - 1)

    def first_of(p):
        return jnp.clip(pair_orbs[p, 0] - me * orbitals, 0, orbitals - 1)

    send_a0.wait_recv()
    send_f0.start()
    get_left.wait()
    get_win0.wait()
    send_p0.wait_recv()
    send_b0.wait_recv()
    send_f0.wait_recv()

    def integrals0(p):
        acc1[p, :, 0:CUT] = -slab_product(left[first_of(p)], win0[second(p)])

    each_pair(integrals0)

    get_x.wait()
    send_amp_x0.wait_recv()
    send_amp_x1.wait_recv()

    def across_first(p):
        q = slot[1, p]
        chosen = jnp.concatenate([amp_x0[q], amp_x1[q]], axis=1)
        acc0[p] += transform(fock[p, column_x], inter_x[p], chosen, 0)

    each_pair(across_first)

    def denominator(p, first, width):
        row = virtual[pl.ds(p, 1), :]
        column = jnp.broadcast_to(row, (128, nv)).T
        if width > 128:
            column = jnp.concatenate([column] * (width // 128), axis=1)
        return column + row[:, first : first + width] - occupied[p]

    def update0(p):
        denom = denominator(p, 0, CUT)
        old = cur[p, :, 0:CUT]
        residual = denom * old - acc1[p, :, 0:CUT] - acc0[p, :, 0:CUT]
        cur[p, :, 0:CUT] = old - residual / denom

    each_pair(update0)

    send_amp_x0.wait_send()
    send_amp_x1.wait_send()
    send_amp_p0.wait_send()
    send_amp_p1.wait_send()
    gather(1, out_x0, 0)
    send_cur_x0.start()
    gather(0, out_p0, 0)
    send_cur_p0.start()

    def own_second0(p):
        chosen = cur[third(p), :, 0:CUT]
        whole = transform(fock[p, 2], inter_own[p], chosen, 0)
        acc1[p, :, 0:CUT] += whole[:, 0:CUT]
        acc1[p, :, CUT:nv] = whole[:, CUT:nv]

    each_pair(own_second0)

    send_a1.wait_recv()
    send_f1.start()
    send_cur_p0.wait_recv()

    def partner_second0(p):
        acc1[p] += transform(fock[p, column_p], inter_p[p], cur_p0[slot[0, p]], 0)

    each_pair(partner_second0)

    get_win1.wait()
    send_p1.wait_recv()
    send_b1.wait_recv()
    send_f1.wait_recv()

    def update1(p):
        product = slab_product(left[first_of(p)], win1[second(p)])
        denom = denominator(p, CUT, nv - CUT)
        old = cur[p, :, CUT:nv]
        residual = product + denom * old - acc0[p, :, CUT:nv]
        cur[p, :, CUT:nv] = old - residual / denom
        acc1[p, :, CUT:nv] -= product

    each_pair(update1)

    gather(1, out_x1, CUT)
    send_cur_x1.start()
    gather(0, out_p1, CUT)
    send_cur_p1.start()

    def own_second1(p):
        chosen = cur[third(p), :, CUT:nv]
        acc1[p] += transform(fock[p, 2], inter_own[p], chosen, CUT)

    each_pair(own_second1)

    send_cur_p1.wait_recv()

    def partner_second1(p):
        acc1[p] += transform(fock[p, column_p], inter_p[p], cur_p1[slot[0, p]], CUT)

    each_pair(partner_second1)

    send_cur_x0.wait_recv()

    def across_second0(p):
        acc1[p] += transform(fock[p, column_x], inter_x[p], cur_x0[slot[1, p]], 0)

    each_pair(across_second0)

    send_cur_x1.wait_recv()

    def store(p):
        return pltpu.make_async_copy(cur.at[p], out.at[p], store_sem.at[p])

    def across_second1(p):
        whole = acc1[p] + transform(fock[p, column_x], inter_x[p], cur_x1[slot[1, p]], CUT)
        denom = denominator(p, 0, nv)
        old = cur[p]
        cur[p] = old - (denom * old - whole) / denom
        store(p).start()

    each_pair(across_second1)

    for copy in (
        send_idx_p,
        send_idx_x,
        send_p0,
        send_p1,
        send_a0,
        send_a1,
        send_b0,
        send_b1,
        send_f0,
        send_f1,
        send_cur_p0,
        send_cur_p1,
        send_cur_x0,
        send_cur_x1,
    ):
        copy.wait_send()
    each_pair(lambda p: store(p).wait())


def shards(
    slabs,
    amplitudes,
    intersections,
    fock_coupling,
    virt_energy,
    occ_pair_energy,
    pair_orbs,
    couplings,
):
    devices = lax.axis_size("orb")
    orbitals, nv, nq = slabs.shape
    pairs = amplitudes.shape[0]
    picks = pairs // 2
    smem = pl.BlockSpec(memory_space=pltpu.SMEM)
    vmem = pl.BlockSpec(memory_space=pltpu.VMEM)
    hbm = pl.BlockSpec(memory_space=pl.ANY)
    block = lambda count, width: pltpu.VMEM((count, nv, width), F32)
    pieces = [block(picks, CUT), block(picks, nv - CUT)]
    return pl.pallas_call(
        functools.partial(kernel, devices),
        out_shape=jax.ShapeDtypeStruct(amplitudes.shape, F32),
        in_specs=[smem, smem, smem, smem, vmem, hbm, hbm, hbm],
        out_specs=hbm,
        scratch_shapes=[
            block(pairs, nv),
            block(pairs, nv),
            block(pairs, nv),
            block(pairs, nv),
            block(pairs, nv),
            block(pairs, nv),
            block(orbitals, nq),
            pltpu.VMEM((5 * orbitals, CUT, nq), F32),
            pltpu.VMEM((5 * orbitals, nv - CUT, nq), F32),
            *(pieces * 6),
            pltpu.SMEM(couplings.shape, jnp.int32),
            pltpu.SMEM(couplings.shape, jnp.int32),
            pltpu.SMEM((2, picks), jnp.int32),
            pltpu.SMEM((2, pairs), jnp.int32),
            pltpu.SemaphoreType.DMA((KINDS,)),
            pltpu.SemaphoreType.DMA((KINDS,)),
            pltpu.SemaphoreType.DMA((7,)),
            pltpu.SemaphoreType.DMA((pairs,)),
        ],
        compiler_params=pltpu.CompilerParams(
            collective_id=0, has_side_effects=True, vmem_limit_bytes=67043328
        ),
        name="amplitudes",
    )(
        couplings,
        pair_orbs,
        fock_coupling,
        occ_pair_energy,
        virt_energy,
        slabs,
        amplitudes,
        intersections,
    )


def solution(mesh):
    in_specs = (
        P("orb", None, None),
        P("orb", None, None),
        P("orb", None, None, None),
        P("orb", None),
        P("orb", None),
        P("orb"),
        P("orb", None),
        P("orb", None),
    )
    out_specs = P("orb", None, None)
    return jax.shard_map(shards, mesh=mesh, in_specs=in_specs, out_specs=out_specs, check_vma=False)
```

time: 542 us -> 158 us (0.29); the launches traced: 536 us -> 157 us
  matrix products: 186 us -> 0 us
  waiting for transfers between devices: 157 us -> 0 us
  Pallas kernels: 0 us -> 149 us
  local copies, waits for them, and re-layouts: 138 us -> 8.9 us
  other arithmetic: 30 us -> 0 us
  starting transfers between devices: 23.5 us -> 0 us
    dot_general x33 -> x0, matrix products: 186 us -> none  [the longest x16 83.3 us: project_pair(): jnp.einsum('cab,cbe->cae', intersection, picked, precision=highest, prefe...]
    ppermute x8 -> x0, waiting for transfers between devices: 157 us -> none  [the longest x4 106 us: shifted(): return lax.ppermute(value, axis, pairs)]
    pallas_call x0 -> x1, Pallas kernels: none -> 149 us  [shards(): pl.pallas_call(functools.partial(kernel, devices), out_shape=jax.ShapeDty...]
    gather x18 -> x0, local copies, waits for them, and re-layouts: 107 us -> none  [the longest x16 90.9 us: project_pair(): picked = jnp.take(nearby, chosen_rows, axis=0)]
    ppermute x8 -> x0, starting transfers between devices: 23.5 us -> none  [the longest x2 14.3 us: with_halo(): lax.ppermute(head, axis, [((i + 1) % count, i) for i in range(count)])]
    concatenate x2 -> x0, other arithmetic: 14.8 us -> none  [with_halo(): jnp.concatenate([lax.ppermute(tail, axis, [(i, (i + 1) % count) for i in...]
    sub x4 -> x0, other arithmetic: 14 us -> none  [the longest x2 14 us: shards(): current = current - residual / denominator]
    dynamic_update_slice x16 -> x0, local copies, waits for them, and re-layouts: 13.9 us -> none  [shards(): lax.map(project_pair, (coupled_index, fock_coupling, intersections))]
  transfers between devices with their start and end apart: 8 -> 0, of which waited for: 3 -> 0; matrix products, arithmetic and copies ran while one was open for 8% -> 0% of each run, Pallas kernels for 0% -> 0%
where the time goes in v1:
time: 158 us; the launch traced here: 157 us
  Pallas kernels  149 us (94%)
  local copies, waits for them, and re-layouts  8.9 us (6%)
    pallas_call x1, Pallas kernels, shards(): pl.pallas_call(functools.partial(kernel, devices), out_shape=jax.ShapeDty...  149 us
    unnamed x4, local copies, waits for them, and re-layouts  8.9 us

profile of v1, /device:TPU:0, one launch (start us, length us, event | category | flops | bytes accessed | tf_op | source)
XLA Modules:
  0.0 157.5 jit_solution(4220065126430881758)
XLA Ops:
  0.0 1.3 copy.11.fock
  1.3 1.3 copy.10.pair_orbs
  2.7 1.3 copy.9.couplings
  4.0 148.6 %amplitudes.2 = f32[8,384,384]{2,1,0:T(8,128)} custom-call(s32[8,3]{1,0:T(8,128)} %copy.9.couplings, s32[8,2]{1,0:T(8,128)} %copy.10.pair_orbs, f32[8,3]{1,0:T(8,128)} %copy.11.fock, f32[8]{0:T(128)} %occupied.1, f32[8,384]{1,0:T(8,128)} %virtual.1, f32[2,384,768]{2,1,0:T(8,128)} %slabs.1, f32[8,384,384]{2,1,0:T(8,128)} %amplitudes.3, ...), custom_call_target="tpu_custom_call" | custom-call | tf_op jit(solution)/shard_map/amplitudes/pallas_call | solution.py:430
  152.6 4.9 %copy.13 = f32[8,384,384]{2,1,0:T(8,128)} copy(f32[8,384,384]{2,1,0:T(8,128)} %amplitudes.2) | data formatting | bytes 9437184

commit v2 on v1

--- a/solution.py
+++ b/solution.py
@@ -13,6 +13,8 @@
 NT = (((1,), (1,)), ((), ()))
 
 CUT = 256
+
+PER_TURN = 2
 
 IDX_P, IDX_X = 0, 1
 SLAB_P = 2
@@ -41,11 +43,17 @@
     return lax.dot_general(a, b, NT, preferred_element_type=F32)
 
 
+def by_halves(dot, a, b):
+    middle = a.shape[0] // 2
+    return jnp.concatenate([dot(a[:middle], b), dot(a[middle:], b)], axis=0)
+
+
 def transform(gain, full, chunk, first):
     width = chunk.shape[1]
     full_hi, full_lo = split(full)
-    chunk_hi, chunk_lo = split(chunk)
-    half = gain * dot_nn(
+    chunk_hi, chunk_lo = split(gain * chunk)
+    half = by_halves(
+        dot_nn,
         jnp.concatenate([full_hi, full_hi, full_lo], axis=1),
         jnp.concatenate([chunk_hi, chunk_lo, chunk_hi], axis=0),
     )
@@ -61,7 +69,11 @@
 def slab_product(left, right):
     left_hi, left_lo = split(left)
     right_hi, right_lo = split(right)
-    return dot_nt(left_hi, right_hi) + dot_nt(left_hi, right_lo) + dot_nt(left_lo, right_hi)
+    return by_halves(
+        dot_nt,
+        jnp.concatenate([left_hi, left_hi, left_lo], axis=1),
+        jnp.concatenate([right_hi, right_lo, right_hi], axis=1),
+    )
 
 
 def kernel(
@@ -74,7 +86,6 @@
     slabs,
     amplitudes,
     intersections,
-    out,
     cur,
     acc0,
     acc1,
@@ -103,7 +114,6 @@
     send_sem,
     recv_sem,
     local_sem,
-    store_sem,
 ):
     pairs, nv = cur.shape[0], cur.shape[1]
     picks = out_p0.shape[0]
@@ -174,12 +184,11 @@
     send_idx_p.start()
     send_a0.start()
     send_b0.start()
-    send_b1.start()
     send_p0.start()
     send_p1.start()
 
     def tables(source, column, base):
-        named = [source[p, column] - base for p in range(pairs)]
+        named = [source[column, p] - base for p in range(pairs)]
         present = []
         for q in range(pairs):
             hit = jnp.int32(0)
@@ -231,20 +240,21 @@
     send_amp_p1.start()
 
     def each_pair(step):
-        def body(p, carry):
-            step(p)
+        def body(turn, carry):
+            for p in range(PER_TURN):
+                step(turn * PER_TURN + p)
             return carry
 
-        lax.fori_loop(0, pairs, body, 0)
+        lax.fori_loop(0, pairs // PER_TURN, body, 0)
 
     def third(p):
-        return jnp.clip(couplings[p, 2] - me * pairs, 0, pairs - 1)
+        return jnp.clip(couplings[2, p] - me * pairs, 0, pairs - 1)
 
     get_own.wait()
 
     def own_first(p):
         chosen = cur[third(p)]
-        acc0[p] = transform(fock[p, 2], inter_own[p], chosen, 0)
+        acc0[p] = transform(fock[2, p], inter_own[p], chosen, 0)
 
     each_pair(own_first)
 
@@ -255,19 +265,19 @@
     def partner_first(p):
         q = slot[0, p]
         chosen = jnp.concatenate([amp_p0[q], amp_p1[q]], axis=1)
-        acc0[p] += transform(fock[p, column_p], inter_p[p], chosen, 0)
+        acc0[p] += transform(fock[column_p, p], inter_p[p], chosen, 0)
 
     each_pair(partner_first)
 
     def second(p):
-        offset = lax.div(pair_orbs[p, 1], orbitals) - me
-        parity = lax.rem(pair_orbs[p, 1], orbitals)
+        offset = lax.div(pair_orbs[1, p], orbitals) - me
+        parity = lax.rem(pair_orbs[1, p], orbitals)
         turned = offset * side
         place = jnp.where(turned >= 0, turned, 2 - turned)
         return jnp.clip(place * orbitals + parity, 0, win0.shape[0] - 1)
 
     def first_of(p):
-        return jnp.clip(pair_orbs[p, 0] - me * orbitals, 0, orbitals - 1)
+        return jnp.clip(pair_orbs[0, p] - me * orbitals, 0, orbitals - 1)
 
     send_a0.wait_recv()
     send_f0.start()
@@ -284,14 +294,19 @@
 
     get_x.wait()
     send_amp_x0.wait_recv()
+
+    def across_first0(p):
+        acc0[p] += transform(fock[column_x, p], inter_x[p], amp_x0[slot[1, p]], 0)
+
+    each_pair(across_first0)
+
     send_amp_x1.wait_recv()
-
-    def across_first(p):
-        q = slot[1, p]
-        chosen = jnp.concatenate([amp_x0[q], amp_x1[q]], axis=1)
-        acc0[p] += transform(fock[p, column_x], inter_x[p], chosen, 0)
-
-    each_pair(across_first)
+    send_b1.start()
+
+    def across_first1(p):
+        acc0[p] += transform(fock[column_x, p], inter_x[p], amp_x1[slot[1, p]], CUT)
+
+    each_pair(across_first1)
 
     def denominator(p, first, width):
         row = virtual[pl.ds(p, 1), :]
@@ -319,7 +334,7 @@
 
     def own_second0(p):
         chosen = cur[third(p), :, 0:CUT]
-        whole = transform(fock[p, 2], inter_own[p], chosen, 0)
+        whole = transform(fock[2, p], inter_own[p], chosen, 0)
         acc1[p, :, 0:CUT] += whole[:, 0:CUT]
         acc1[p, :, CUT:nv] = whole[:, CUT:nv]
 
@@ -330,7 +345,7 @@
     send_cur_p0.wait_recv()
 
     def partner_second0(p):
-        acc1[p] += transform(fock[p, column_p], inter_p[p], cur_p0[slot[0, p]], 0)
+        acc1[p] += transform(fock[column_p, p], inter_p[p], cur_p0[slot[0, p]], 0)
 
     each_pair(partner_second0)
 
@@ -356,35 +371,31 @@
 
     def own_second1(p):
         chosen = cur[third(p), :, CUT:nv]
-        acc1[p] += transform(fock[p, 2], inter_own[p], chosen, CUT)
+        acc1[p] += transform(fock[2, p], inter_own[p], chosen, CUT)
 
     each_pair(own_second1)
 
     send_cur_p1.wait_recv()
 
     def partner_second1(p):
-        acc1[p] += transform(fock[p, column_p], inter_p[p], cur_p1[slot[0, p]], CUT)
+        acc1[p] += transform(fock[column_p, p], inter_p[p], cur_p1[slot[0, p]], CUT)
 
     each_pair(partner_second1)
 
     send_cur_x0.wait_recv()
 
     def across_second0(p):
-        acc1[p] += transform(fock[p, column_x], inter_x[p], cur_x0[slot[1, p]], 0)
+        acc1[p] += transform(fock[column_x, p], inter_x[p], cur_x0[slot[1, p]], 0)
 
     each_pair(across_second0)
 
     send_cur_x1.wait_recv()
 
-    def store(p):
-        return pltpu.make_async_copy(cur.at[p], out.at[p], store_sem.at[p])
-
     def across_second1(p):
-        whole = acc1[p] + transform(fock[p, column_x], inter_x[p], cur_x1[slot[1, p]], CUT)
+        whole = acc1[p] + transform(fock[column_x, p], inter_x[p], cur_x1[slot[1, p]], CUT)
         denom = denominator(p, 0, nv)
         old = cur[p]
         cur[p] = old - (denom * old - whole) / denom
-        store(p).start()
 
     each_pair(across_second1)
 
@@ -405,7 +416,6 @@
         send_cur_x1,
     ):
         copy.wait_send()
-    each_pair(lambda p: store(p).wait())
 
 
 def shards(
@@ -429,11 +439,10 @@
     pieces = [block(picks, CUT), block(picks, nv - CUT)]
     return pl.pallas_call(
         functools.partial(kernel, devices),
-        out_shape=jax.ShapeDtypeStruct(amplitudes.shape, F32),
+        out_shape=pltpu.VMEM(amplitudes.shape, F32),
         in_specs=[smem, smem, smem, smem, vmem, hbm, hbm, hbm],
-        out_specs=hbm,
+        out_specs=vmem,
         scratch_shapes=[
-            block(pairs, nv),
             block(pairs, nv),
             block(pairs, nv),
             block(pairs, nv),
@@ -443,23 +452,22 @@
             pltpu.VMEM((5 * orbitals, CUT, nq), F32),
             pltpu.VMEM((5 * orbitals, nv - CUT, nq), F32),
             *(pieces * 6),
-            pltpu.SMEM(couplings.shape, jnp.int32),
-            pltpu.SMEM(couplings.shape, jnp.int32),
+            pltpu.SMEM(couplings.shape[::-1], jnp.int32),
+            pltpu.SMEM(couplings.shape[::-1], jnp.int32),
             pltpu.SMEM((2, picks), jnp.int32),
             pltpu.SMEM((2, pairs), jnp.int32),
             pltpu.SemaphoreType.DMA((KINDS,)),
             pltpu.SemaphoreType.DMA((KINDS,)),
             pltpu.SemaphoreType.DMA((7,)),
-            pltpu.SemaphoreType.DMA((pairs,)),
         ],
         compiler_params=pltpu.CompilerParams(
-            collective_id=0, has_side_effects=True, vmem_limit_bytes=67043328
+            collective_id=0, has_side_effects=True, vmem_limit_bytes=62000000
         ),
         name="amplitudes",
     )(
-        couplings,
-        pair_orbs,
-        fock_coupling,
+        couplings.T,
+        pair_orbs.T,
+        fock_coupling.T,
         occ_pair_energy,
         virt_energy,
         slabs,

time: 158 us -> 121 us (0.77)
  Pallas kernels: 149 us -> 119 us
  local copies, waits for them, and re-layouts: 8.9 us -> 2.19 us
    pallas_call x1, Pallas kernels: 149 us -> 119 us  [shards(): pl.pallas_call(functools.partial(kernel, devices), out_shape=pltpu.VMEM(a...]
    unnamed x4 -> x1, local copies, waits for them, and re-layouts: 8.9 us -> 2.19 us
where the time goes in v2:
time: 121 us
  Pallas kernels  119 us (98%)
  local copies, waits for them, and re-layouts  2.19 us (2%)
    pallas_call x1, Pallas kernels, shards(): pl.pallas_call(functools.partial(kernel, devices), out_shape=pltpu.VMEM(a...  119 us

profile of v2, /device:TPU:0, one launch (start us, length us, event | category | flops | bytes accessed | tf_op | source)
XLA Modules:
  0.0 121.2 jit_solution(17695608888516903109)
XLA Ops:
  0.0 119.0 %amplitudes.2 = f32[8,384,384]{2,1,0:T(8,128)S(1)} custom-call(s32[3,8]{1,0:T(4,128)} %bitcast.3, s32[2,8]{1,0:T(2,128)} %bitcast.5, f32[3,8]{1,0:T(4,128)} %bitcast.4, f32[8]{0:T(128)} %occupied.1, f32[8,384]{1,0:T(8,128)} %virtual.1, f32[2,384,768]{2,1,0:T(8,128)} %slabs.1, f32[8,384,384]{2,1,0:T(8,128)} %amplitudes.3, f32[8,3,384,384]{3,2,1,0:T(8,128)} %intersections.1), custom_call_target="tpu_custom_call" | custom-call | tf_op jit(solution)/shard_map/amplitudes/pallas_call | solution.py:440
  119.0 2.2 %copy.10 = f32[8,384,384]{2,1,0:T(8,128)} copy(f32[8,384,384]{2,1,0:T(8,128)S(1)} %amplitudes.2) | data formatting | bytes 9437184

commit v3 on v2

--- a/solution.py
+++ b/solution.py
@@ -14,7 +14,7 @@
 
 CUT = 256
 
-PER_TURN = 2
+PER_TURN = 4
 
 IDX_P, IDX_X = 0, 1
 SLAB_P = 2
@@ -25,7 +25,8 @@
 AMP_X = 12
 CUR_P = 14
 CUR_X = 16
-KINDS = 18
+CUR_X_LAST = 18
+KINDS = 19
 
 OWN, PARTNER, FORWARDED, ACROSS, ACROSS2 = 0, 2, 4, 6, 8
 
@@ -46,23 +47,59 @@
 def by_halves(dot, a, b):
     middle = a.shape[0] // 2
     return jnp.concatenate([dot(a[:middle], b), dot(a[middle:], b)], axis=0)
+
+
+def wide_half(full_hi, full_lo, chunk_hi, chunk_lo):
+    return by_halves(
+        dot_nn,
+        jnp.concatenate([full_hi, full_hi, full_lo], axis=1),
+        jnp.concatenate([chunk_hi, chunk_lo, chunk_hi], axis=0),
+    )
+
+
+def folded(product):
+    width = product.shape[1] // 2
+    return product[:, :width] + product[:, width:]
+
+
+def narrow_half_upper(full_hi, full_lo, chunk_hi, chunk_lo):
+    both = by_halves(dot_nn, full_hi, jnp.concatenate([chunk_hi, chunk_lo], axis=1))
+    return folded(both) + by_halves(dot_nn, full_lo, chunk_hi)
+
+
+def narrow_half_lower(full_hi, full_lo, chunk_hi, chunk_lo):
+    upper = jnp.concatenate([chunk_hi, chunk_lo], axis=1)
+    lower = jnp.concatenate([chunk_hi, jnp.zeros_like(chunk_lo)], axis=1)
+    return folded(
+        by_halves(
+            dot_nn,
+            jnp.concatenate([full_hi, full_lo], axis=1),
+            jnp.concatenate([upper, lower], axis=0),
+        )
+    )
+
+
+def second_product(half, part_hi, part_lo):
+    half_hi, half_lo = split(half)
+    return by_halves(
+        dot_nt,
+        jnp.concatenate([half_hi, half_hi, half_lo], axis=1),
+        jnp.concatenate([part_hi, part_lo, part_hi], axis=1),
+    )
 
 
 def transform(gain, full, chunk, first):
     width = chunk.shape[1]
     full_hi, full_lo = split(full)
     chunk_hi, chunk_lo = split(gain * chunk)
-    half = by_halves(
-        dot_nn,
-        jnp.concatenate([full_hi, full_hi, full_lo], axis=1),
-        jnp.concatenate([chunk_hi, chunk_lo, chunk_hi], axis=0),
-    )
-    half_hi, half_lo = split(half)
-    part_hi = full_hi[:, first : first + width]
-    part_lo = full_lo[:, first : first + width]
-    return dot_nt(
-        jnp.concatenate([half_hi, half_hi, half_lo], axis=1),
-        jnp.concatenate([part_hi, part_lo, part_hi], axis=1),
+    if width > 128:
+        half = wide_half(full_hi, full_lo, chunk_hi, chunk_lo)
+    else:
+        half = narrow_half_upper(
+            full_hi[:, :CUT], full_lo[:, :CUT], chunk_hi[:CUT], chunk_lo[:CUT]
+        ) + narrow_half_lower(full_hi[:, CUT:], full_lo[:, CUT:], chunk_hi[CUT:], chunk_lo[CUT:])
+    return second_product(
+        half, full_hi[:, first : first + width], full_lo[:, first : first + width]
     )
 
 
@@ -102,7 +139,8 @@
     cur_p0,
     cur_p1,
     cur_x0,
-    cur_x1,
+    cur_x1a,
+    cur_x1b,
     out_p0,
     out_p1,
     out_x0,
@@ -111,9 +149,11 @@
     idx_x,
     pick,
     slot,
+    halves,
     send_sem,
     recv_sem,
     local_sem,
+    fill_sem,
 ):
     pairs, nv = cur.shape[0], cur.shape[1]
     picks = out_p0.shape[0]
@@ -143,10 +183,27 @@
     get_win1 = fetch(slabs.at[:, pl.ds(CUT, nv - CUT)], win1.at[pl.ds(OWN, orbitals)])
     get_x = fetch(intersections.at[:, column_x], inter_x)
 
+    sends_across = jnp.logical_and(me != devices - 1, me != 0)
+    sends_two_across = jnp.logical_and(me != devices - 2, me != 1)
+    gets_across = jnp.logical_and(me != 0, me != devices - 1)
+    gets_forwarded = jnp.logical_and(me != 1, me != devices - 2)
+
+    def choose(found, then, otherwise=None):
+        pl.when(found)(then)
+        if otherwise is not None:
+            pl.when(jnp.logical_not(found))(otherwise)
+
     barrier = pltpu.get_barrier_semaphore()
-    for other in (partner, across, target2, source2):
+
+    def greet(other):
         pl.semaphore_signal(barrier, inc=1, device_id=(other,), device_id_type=MESH)
-    pl.semaphore_wait(barrier, 4)
+
+    greet(partner)
+    greet(across)
+    choose(sends_two_across, lambda: greet(target2))
+    choose(gets_across, lambda: greet(source2))
+    greeted = 2 + sends_two_across.astype(jnp.int32) + gets_across.astype(jnp.int32)
+    pl.semaphore_wait(barrier, greeted)
 
     def remote(src, dst, kind, device):
         return pltpu.make_async_remote_copy(
@@ -161,6 +218,12 @@
     slab0 = slabs.at[:, pl.ds(0, CUT)]
     slab1 = slabs.at[:, pl.ds(CUT, nv - CUT)]
     rows = lambda first: pl.ds(first, orbitals)
+    def fill(src, window, *places):
+        for place in places:
+            copy = pltpu.make_async_copy(src, window.at[rows(place)], fill_sem)
+            copy.start()
+            copy.wait()
+
     send_idx_p = remote(couplings, idx_p, IDX_P, partner)
     send_idx_x = remote(couplings, idx_x, IDX_X, across)
     send_p0 = remote(slab0, win0.at[rows(PARTNER)], SLAB_P, partner)
@@ -178,12 +241,13 @@
     send_cur_p0 = remote(out_p0, cur_p0, CUR_P, partner)
     send_cur_p1 = remote(out_p1, cur_p1, CUR_P + 1, partner)
     send_cur_x0 = remote(out_x0, cur_x0, CUR_X, across)
-    send_cur_x1 = remote(out_x1, cur_x1, CUR_X + 1, across)
+    send_cur_x1a = remote(out_x1.at[:, pl.ds(0, CUT)], cur_x1a, CUR_X + 1, across)
+    send_cur_x1b = remote(out_x1.at[:, pl.ds(CUT, nv - CUT)], cur_x1b, CUR_X_LAST, across)
 
     send_idx_x.start()
     send_idx_p.start()
-    send_a0.start()
-    send_b0.start()
+    choose(sends_across, send_a0.start)
+    choose(sends_two_across, send_b0.start)
     send_p0.start()
     send_p1.start()
 
@@ -233,7 +297,7 @@
     gather(1, out_x1, CUT)
     send_amp_x0.start()
     send_amp_x1.start()
-    send_a1.start()
+    choose(sends_across, send_a1.start)
     gather(0, out_p0, 0)
     gather(0, out_p1, CUT)
     send_amp_p0.start()
@@ -279,13 +343,16 @@
     def first_of(p):
         return jnp.clip(pair_orbs[0, p] - me * orbitals, 0, orbitals - 1)
 
-    send_a0.wait_recv()
-    send_f0.start()
+    def forward0():
+        send_a0.wait_recv()
+        send_f0.start()
+
+    choose(gets_across, forward0)
     get_left.wait()
     get_win0.wait()
     send_p0.wait_recv()
-    send_b0.wait_recv()
-    send_f0.wait_recv()
+    choose(gets_across, send_b0.wait_recv, lambda: fill(slab0, win0, ACROSS, ACROSS2))
+    choose(gets_forwarded, send_f0.wait_recv, lambda: fill(slab0, win0, FORWARDED))
 
     def integrals0(p):
         acc1[p, :, 0:CUT] = -slab_product(left[first_of(p)], win0[second(p)])
@@ -301,7 +368,7 @@
     each_pair(across_first0)
 
     send_amp_x1.wait_recv()
-    send_b1.start()
+    choose(sends_two_across, send_b1.start)
 
     def across_first1(p):
         acc0[p] += transform(fock[column_x, p], inter_x[p], amp_x1[slot[1, p]], CUT)
@@ -340,8 +407,11 @@
 
     each_pair(own_second0)
 
-    send_a1.wait_recv()
-    send_f1.start()
+    def forward1():
+        send_a1.wait_recv()
+        send_f1.start()
+
+    choose(gets_across, forward1)
     send_cur_p0.wait_recv()
 
     def partner_second0(p):
@@ -351,8 +421,8 @@
 
     get_win1.wait()
     send_p1.wait_recv()
-    send_b1.wait_recv()
-    send_f1.wait_recv()
+    choose(gets_across, send_b1.wait_recv, lambda: fill(slab1, win1, ACROSS, ACROSS2))
+    choose(gets_forwarded, send_f1.wait_recv, lambda: fill(slab1, win1, FORWARDED))
 
     def update1(p):
         product = slab_product(left[first_of(p)], win1[second(p)])
@@ -365,7 +435,8 @@
     each_pair(update1)
 
     gather(1, out_x1, CUT)
-    send_cur_x1.start()
+    send_cur_x1a.start()
+    send_cur_x1b.start()
     gather(0, out_p1, CUT)
     send_cur_p1.start()
 
@@ -389,33 +460,56 @@
 
     each_pair(across_second0)
 
-    send_cur_x1.wait_recv()
-
-    def across_second1(p):
-        whole = acc1[p] + transform(fock[column_x, p], inter_x[p], cur_x1[slot[1, p]], CUT)
+    send_cur_x1a.wait_recv()
+
+    def across_second1a(p):
+        full_hi, full_lo = split(inter_x[p, :, 0:CUT])
+        chunk_hi, chunk_lo = split(fock[column_x, p] * cur_x1a[slot[1, p]])
+        halves[p] = narrow_half_upper(full_hi, full_lo, chunk_hi, chunk_lo)
+
+    each_pair(across_second1a)
+
+    send_cur_x1b.wait_recv()
+
+    def across_second1b(p):
+        full_hi, full_lo = split(inter_x[p, :, CUT:nv])
+        chunk_hi, chunk_lo = split(fock[column_x, p] * cur_x1b[slot[1, p]])
+        half = halves[p] + narrow_half_lower(full_hi, full_lo, chunk_hi, chunk_lo)
+        whole = acc1[p] + second_product(half, full_hi, full_lo)
         denom = denominator(p, 0, nv)
         old = cur[p]
         cur[p] = old - (denom * old - whole) / denom
 
-    each_pair(across_second1)
+    each_pair(across_second1b)
 
     for copy in (
         send_idx_p,
         send_idx_x,
         send_p0,
         send_p1,
-        send_a0,
-        send_a1,
-        send_b0,
-        send_b1,
-        send_f0,
-        send_f1,
         send_cur_p0,
         send_cur_p1,
         send_cur_x0,
-        send_cur_x1,
+        send_cur_x1a,
+        send_cur_x1b,
     ):
         copy.wait_send()
+
+    def sent_across():
+        send_a0.wait_send()
+        send_a1.wait_send()
+
+    def sent_two_across():
+        send_b0.wait_send()
+        send_b1.wait_send()
+
+    def sent_forwarded():
+        send_f0.wait_send()
+        send_f1.wait_send()
+
+    choose(sends_across, sent_across)
+    choose(sends_two_across, sent_two_across)
+    choose(gets_across, sent_forwarded)
 
 
 def shards(
@@ -451,14 +545,20 @@
             block(orbitals, nq),
             pltpu.VMEM((5 * orbitals, CUT, nq), F32),
             pltpu.VMEM((5 * orbitals, nv - CUT, nq), F32),
-            *(pieces * 6),
+            *(pieces * 3),
+            pieces[0],
+            pltpu.VMEM((picks, CUT, nv - CUT), F32),
+            pltpu.VMEM((picks, nv - CUT, nv - CUT), F32),
+            *(pieces * 2),
             pltpu.SMEM(couplings.shape[::-1], jnp.int32),
             pltpu.SMEM(couplings.shape[::-1], jnp.int32),
             pltpu.SMEM((2, picks), jnp.int32),
             pltpu.SMEM((2, pairs), jnp.int32),
+            block(pairs, nv - CUT),
             pltpu.SemaphoreType.DMA((KINDS,)),
             pltpu.SemaphoreType.DMA((KINDS,)),
             pltpu.SemaphoreType.DMA((7,)),
+            pltpu.SemaphoreType.DMA,
         ],
         compiler_params=pltpu.CompilerParams(
             collective_id=0, has_side_effects=True, vmem_limit_bytes=62000000

time: 121 us -> 116 us (0.959)
  the two profiles are of different devices: /device:TPU:0 before, /device:TPU:95 now
where the time goes in v3:
time: 116 us
  Pallas kernels  114 us (98%)
  local copies, waits for them, and re-layouts  2.19 us (2%)
    pallas_call x1, Pallas kernels, shards(): pl.pallas_call(functools.partial(kernel, devices), out_shape=pltpu.VMEM(a...  114 us

profile of v3, /device:TPU:95, one launch (start us, length us, event | category | flops | bytes accessed | tf_op | source)
XLA Modules:
  0.0 115.7 jit_solution(5122568494375689491)
XLA Ops:
  0.0 113.5 %amplitudes.2 = f32[8,384,384]{2,1,0:T(8,128)S(1)} custom-call(s32[3,8]{1,0:T(4,128)} %bitcast.3, s32[2,8]{1,0:T(2,128)} %bitcast.5, f32[3,8]{1,0:T(4,128)} %bitcast.4, f32[8]{0:T(128)} %occupied.1, f32[8,384]{1,0:T(8,128)} %virtual.1, f32[2,384,768]{2,1,0:T(8,128)} %slabs.1, f32[8,384,384]{2,1,0:T(8,128)} %amplitudes.3, f32[8,3,384,384]{3,2,1,0:T(8,128)} %intersections.1), custom_call_target="tpu_custom_call" | custom-call | tf_op jit(solution)/shard_map/amplitudes/pallas_call | solution.py:534
  113.6 2.2 %copy.10 = f32[8,384,384]{2,1,0:T(8,128)} copy(f32[8,384,384]{2,1,0:T(8,128)S(1)} %amplitudes.2) | data formatting | bytes 9437184

commit v4 on v3

--- a/solution.py
+++ b/solution.py
@@ -115,20 +115,26 @@
 
 def kernel(
     devices,
+    couplings_hbm,
+    pair_orbs_hbm,
+    fock_hbm,
+    occupied_hbm,
+    virtual_hbm,
+    slabs,
+    amplitudes,
+    intersections,
+    acc1,
+    inter_own,
+    inter_x,
+    halves,
+    cur,
     couplings,
     pair_orbs,
     fock,
     occupied,
     virtual,
-    slabs,
-    amplitudes,
-    intersections,
-    cur,
     acc0,
-    acc1,
-    inter_own,
     inter_p,
-    inter_x,
     left,
     win0,
     win1,
@@ -149,7 +155,6 @@
     idx_x,
     pick,
     slot,
-    halves,
     send_sem,
     recv_sem,
     local_sem,
@@ -167,6 +172,25 @@
     column_p = lax.rem(me + 1, 2)
     column_x = lax.rem(me, 2)
 
+    sends_across = jnp.logical_and(me != devices - 1, me != 0)
+    sends_two_across = jnp.logical_and(me != devices - 2, me != 1)
+    gets_across = jnp.logical_and(me != 0, me != devices - 1)
+    gets_forwarded = jnp.logical_and(me != 1, me != devices - 2)
+
+    def choose(found, then, otherwise=None):
+        pl.when(found)(then)
+        if otherwise is not None:
+            pl.when(jnp.logical_not(found))(otherwise)
+
+    barrier = pltpu.get_barrier_semaphore()
+
+    def greet(other):
+        pl.semaphore_signal(barrier, inc=1, device_id=(other,), device_id_type=MESH)
+
+    greet(partner)
+    greet(across)
+    choose(sends_two_across, lambda: greet(target2))
+    choose(gets_across, lambda: greet(source2))
     local = []
 
     def fetch(src, dst):
@@ -175,33 +199,9 @@
         copy.start()
         return copy
 
+    get_couplings = fetch(couplings_hbm, couplings)
     get_cur = fetch(amplitudes, cur)
-    get_own = fetch(intersections.at[:, 2], inter_own)
-    get_p = fetch(intersections.at[:, column_p], inter_p)
-    get_left = fetch(slabs, left)
-    get_win0 = fetch(slabs.at[:, pl.ds(0, CUT)], win0.at[pl.ds(OWN, orbitals)])
-    get_win1 = fetch(slabs.at[:, pl.ds(CUT, nv - CUT)], win1.at[pl.ds(OWN, orbitals)])
-    get_x = fetch(intersections.at[:, column_x], inter_x)
-
-    sends_across = jnp.logical_and(me != devices - 1, me != 0)
-    sends_two_across = jnp.logical_and(me != devices - 2, me != 1)
-    gets_across = jnp.logical_and(me != 0, me != devices - 1)
-    gets_forwarded = jnp.logical_and(me != 1, me != devices - 2)
-
-    def choose(found, then, otherwise=None):
-        pl.when(found)(then)
-        if otherwise is not None:
-            pl.when(jnp.logical_not(found))(otherwise)
-
-    barrier = pltpu.get_barrier_semaphore()
-
-    def greet(other):
-        pl.semaphore_signal(barrier, inc=1, device_id=(other,), device_id_type=MESH)
-
-    greet(partner)
-    greet(across)
-    choose(sends_two_across, lambda: greet(target2))
-    choose(gets_across, lambda: greet(source2))
+
     greeted = 2 + sends_two_across.astype(jnp.int32) + gets_across.astype(jnp.int32)
     pl.semaphore_wait(barrier, greeted)
 
@@ -218,14 +218,15 @@
     slab0 = slabs.at[:, pl.ds(0, CUT)]
     slab1 = slabs.at[:, pl.ds(CUT, nv - CUT)]
     rows = lambda first: pl.ds(first, orbitals)
+
     def fill(src, window, *places):
         for place in places:
             copy = pltpu.make_async_copy(src, window.at[rows(place)], fill_sem)
             copy.start()
             copy.wait()
 
-    send_idx_p = remote(couplings, idx_p, IDX_P, partner)
-    send_idx_x = remote(couplings, idx_x, IDX_X, across)
+    send_idx_p = remote(couplings_hbm, idx_p, IDX_P, partner)
+    send_idx_x = remote(couplings_hbm, idx_x, IDX_X, across)
     send_p0 = remote(slab0, win0.at[rows(PARTNER)], SLAB_P, partner)
     send_p1 = remote(slab1, win1.at[rows(PARTNER)], SLAB_P + 1, partner)
     send_a0 = remote(slab0, win0.at[rows(ACROSS)], SLAB_A, across)
@@ -251,6 +252,17 @@
     send_p0.start()
     send_p1.start()
 
+    get_own = fetch(intersections.at[:, 2], inter_own)
+    get_p = fetch(intersections.at[:, column_p], inter_p)
+    get_left = fetch(slabs, left)
+    get_win0 = fetch(slabs.at[:, pl.ds(0, CUT)], win0.at[pl.ds(OWN, orbitals)])
+    get_win1 = fetch(slabs.at[:, pl.ds(CUT, nv - CUT)], win1.at[pl.ds(OWN, orbitals)])
+    get_x = fetch(intersections.at[:, column_x], inter_x)
+    get_fock = fetch(fock_hbm, fock)
+    get_pair_orbs = fetch(pair_orbs_hbm, pair_orbs)
+    get_occupied = fetch(occupied_hbm, occupied)
+    get_virtual = fetch(virtual_hbm, virtual)
+
     def tables(source, column, base):
         named = [source[column, p] - base for p in range(pairs)]
         present = []
@@ -264,6 +276,7 @@
             below.append(below[-1] + present[q])
         return named, present, below
 
+    get_couplings.wait()
     for row, column, owner in ((0, column_p, partner), (1, column_x, across)):
         named, present, below = tables(couplings, column, owner * pairs)
         for p in range(pairs):
@@ -315,6 +328,7 @@
         return jnp.clip(couplings[2, p] - me * pairs, 0, pairs - 1)
 
     get_own.wait()
+    get_fock.wait()
 
     def own_first(p):
         chosen = cur[third(p)]
@@ -349,6 +363,7 @@
 
     choose(gets_across, forward0)
     get_left.wait()
+    get_pair_orbs.wait()
     get_win0.wait()
     send_p0.wait_recv()
     choose(gets_across, send_b0.wait_recv, lambda: fill(slab0, win0, ACROSS, ACROSS2))
@@ -388,6 +403,8 @@
         residual = denom * old - acc1[p, :, 0:CUT] - acc0[p, :, 0:CUT]
         cur[p, :, 0:CUT] = old - residual / denom
 
+    get_occupied.wait()
+    get_virtual.wait()
     each_pair(update0)
 
     send_amp_x0.wait_send()
@@ -456,7 +473,12 @@
     send_cur_x0.wait_recv()
 
     def across_second0(p):
-        acc1[p] += transform(fock[column_x, p], inter_x[p], cur_x0[slot[1, p]], 0)
+        whole = acc1[p] + transform(fock[column_x, p], inter_x[p], cur_x0[slot[1, p]], 0)
+        denom = denominator(p, 0, nv)
+        inverse = 1.0 / denom
+        old = cur[p]
+        acc1[p] = old - (denom * old - whole) * inverse
+        inter_own[p] = inverse
 
     each_pair(across_second0)
 
@@ -474,11 +496,7 @@
     def across_second1b(p):
         full_hi, full_lo = split(inter_x[p, :, CUT:nv])
         chunk_hi, chunk_lo = split(fock[column_x, p] * cur_x1b[slot[1, p]])
-        half = halves[p] + narrow_half_lower(full_hi, full_lo, chunk_hi, chunk_lo)
-        whole = acc1[p] + second_product(half, full_hi, full_lo)
-        denom = denominator(p, 0, nv)
-        old = cur[p]
-        cur[p] = old - (denom * old - whole) / denom
+        halves[p] += narrow_half_lower(full_hi, full_lo, chunk_hi, chunk_lo)
 
     each_pair(across_second1b)
 
@@ -510,6 +528,25 @@
     choose(sends_across, sent_across)
     choose(sends_two_across, sent_two_across)
     choose(gets_across, sent_forwarded)
+
+
+def finish(acc, inverse, inter, halves, out, held, sems):
+    pairs = held.shape[0]
+
+    def put(p):
+        return pltpu.make_async_copy(held.at[p], out.at[p], sems.at[p])
+
+    def body(turn, carry):
+        for step in range(2):
+            p = turn * 2 + step
+            part_hi, part_lo = split(inter[p, :, CUT:])
+            held[p] = acc[p] + second_product(halves[p], part_hi, part_lo) * inverse[p]
+            put(p).start()
+        return carry
+
+    lax.fori_loop(0, pairs // 2, body, 0)
+    for p in range(pairs):
+        put(p).wait()
 
 
 def shards(
@@ -526,20 +563,22 @@
     orbitals, nv, nq = slabs.shape
     pairs = amplitudes.shape[0]
     picks = pairs // 2
-    smem = pl.BlockSpec(memory_space=pltpu.SMEM)
     vmem = pl.BlockSpec(memory_space=pltpu.VMEM)
     hbm = pl.BlockSpec(memory_space=pl.ANY)
     block = lambda count, width: pltpu.VMEM((count, nv, width), F32)
     pieces = [block(picks, CUT), block(picks, nv - CUT)]
-    return pl.pallas_call(
+    kept = pl.pallas_call(
         functools.partial(kernel, devices),
-        out_shape=pltpu.VMEM(amplitudes.shape, F32),
-        in_specs=[smem, smem, smem, smem, vmem, hbm, hbm, hbm],
-        out_specs=vmem,
+        out_shape=[block(pairs, nv)] * 3 + [block(pairs, nv - CUT)],
+        in_specs=[hbm] * 8,
+        out_specs=[vmem] * 4,
         scratch_shapes=[
             block(pairs, nv),
-            block(pairs, nv),
-            block(pairs, nv),
+            pltpu.SMEM(couplings.shape[::-1], jnp.int32),
+            pltpu.SMEM(pair_orbs.shape[::-1], jnp.int32),
+            pltpu.SMEM(fock_coupling.shape[::-1], F32),
+            pltpu.SMEM(occ_pair_energy.shape, F32),
+            pltpu.VMEM(virt_energy.shape, F32),
             block(pairs, nv),
             block(pairs, nv),
             block(orbitals, nq),
@@ -554,14 +593,13 @@
             pltpu.SMEM(couplings.shape[::-1], jnp.int32),
             pltpu.SMEM((2, picks), jnp.int32),
             pltpu.SMEM((2, pairs), jnp.int32),
-            block(pairs, nv - CUT),
             pltpu.SemaphoreType.DMA((KINDS,)),
             pltpu.SemaphoreType.DMA((KINDS,)),
-            pltpu.SemaphoreType.DMA((7,)),
+            pltpu.SemaphoreType.DMA((12,)),
             pltpu.SemaphoreType.DMA,
         ],
         compiler_params=pltpu.CompilerParams(
-            collective_id=0, has_side_effects=True, vmem_limit_bytes=62000000
+            collective_id=0, has_side_effects=True, vmem_limit_bytes=51300000
         ),
         name="amplitudes",
     )(
@@ -574,6 +612,15 @@
         amplitudes,
         intersections,
     )
+    return pl.pallas_call(
+        finish,
+        out_shape=jax.ShapeDtypeStruct(amplitudes.shape, F32),
+        in_specs=[vmem] * 4,
+        out_specs=hbm,
+        scratch_shapes=[block(pairs, nv), pltpu.SemaphoreType.DMA((pairs,))],
+        compiler_params=pltpu.CompilerParams(vmem_limit_bytes=32 << 20),
+        name="finish",
+    )(*kept)
 
 
 def solution(mesh):

time: 116 us -> 116 us (level)
  local copies, waits for them, and re-layouts: 2.19 us -> 0 us
    unnamed x1 -> x0, local copies, waits for them, and re-layouts: 2.19 us -> none
    pallas_call x1 -> x2, Pallas kernels: 114 us -> 115 us  [the longest x1 112 us: shards(): pl.pallas_call(functools.partial(kernel, devices), out_shape=[block(pairs...]
where the time goes in v4:
time: 116 us; the launch traced here: 115 us
  Pallas kernels  115 us (99%)
    pallas_call x1, Pallas kernels, shards(): pl.pallas_call(functools.partial(kernel, devices), out_shape=[block(pairs...  112 us
    pallas_call x1, Pallas kernels, shards(): pl.pallas_call(finish, out_shape=jax.ShapeDtypeStruct(amplitudes.shape, F...  3.41 us

profile of v4, /device:TPU:95, one launch (start us, length us, event | category | flops | bytes accessed | tf_op | source)
XLA Modules:
  0.0 115.3 jit_solution(10277484195968919116)
XLA Ops:
  0.0 111.7 %amplitudes.2 = (f32[8,384,384]{2,1,0:T(8,128)S(1)}, f32[8,384,384]{2,1,0:T(8,128)S(1)}, f32[8,384,384]{2,1,0:T(8,128)S(1)}, f32[8,384,128]{2,1,0:T(8,128)S(1)}) custom-call(s32[3,8]{1,0:T(4,128)} %bitcast.3, s32[2,8]{1,0:T(2,128)} %bitcast.5, f32[3,8]{1,0:T(4,128)} %bitcast.4, f32[8]{0:T(128)} %occupied_hbm.1, f32[8,384]{1,0:T(8,128)} %virtual_hbm.1, ...), custom_call_target="tpu_custom_call" | custom-call | tf_op jit(solution)/shard_map/amplitudes/pallas_call | solution.py:570
  111.7 3.4 %finish.1 = f32[8,384,384]{2,1,0:T(8,128)} custom-call(f32[8,384,384]{2,1,0:T(8,128)S(1)} %get-tuple-element.9.acc, f32[8,384,384]{2,1,0:T(8,128)S(1)} %get-tuple-element.10.inverse, f32[8,384,384]{2,1,0:T(8,128)S(1)} %get-tuple-element.11.inter, f32[8,384,128]{2,1,0:T(8,128)S(1)} %get-tuple-element.12.halves), custom_call_target="tpu_custom_call" | custom-call | tf_op jit(solution)/shard_map/finish/pallas_call | solution.py:615
